TPU v7x, 256 devices: a whole 4x4x8 slice. The times are simulated.
256 devices in a mesh: req: 32 (over y, x, core), head: 8 (over z).
Axes of the slice: x: 4, y: 4, z: 8, core: 2. Of those that a mesh axis runs over, the one named last changes fastest.
Arguments:
- tokens: bfloat16 [4096, 1536], P(('req', 'head')), may hold values from -6 to 6
- pre_gain: float32 [1536], replicated, may hold values from 0.1 to 1.9
- inner_weight: bfloat16 [1536, 2, 3072], P(None, None, 'head')
- shared_weight: bfloat16 [1536, 304], replicated, may hold values from -0.15625 to 0.15625
- conv_inner: float32 [4, 3072], P(None, 'head'), may hold values from -0.5 to 0.5
- conv_inner_bias: float32 [3072], P('head'), may hold values from -0.5 to 0.5
- conv_shared: float32 [4, 256], replicated, may hold values from -0.5 to 0.5
- conv_shared_bias: float32 [256], replicated, may hold values from -0.5 to 0.5
- step_bias: float32 [48], P('head'), may hold values from -4 to 0
- decay_log: float32 [48], P('head'), may hold values from 0 to 2.77
- skip_gain: float32 [48], P('head'), may hold values from 0.5 to 1.5
- gate_gain: float32 [3072], P('head'), may hold values from 0.1 to 1.9
- out_weight: bfloat16 [3072, 1536], P('head'), may hold values from -0.109375 to 0.109375
- states: bfloat16 [1024, 48, 64, 128], P('req', 'head'), may hold values from -1.1953125 to 1.1953125
- edge_inner: bfloat16 [1024, 3, 3072], P('req', None, 'head'), may hold values from -6 to 6
- edge_shared: bfloat16 [1024, 3, 256], P('req'), may hold values from -6 to 6
- counts: int32 [1024], P('req'), may hold values from 1 to 4, as said below
- mig_ids: int32 [32], replicated, may hold values from 0 to 1023, as said below
- mig_dest: int32 [32], replicated, may hold values from 0 to 1023, as said below
- reorder: int32 [1024], replicated, may hold values from 0 to 1023, as said below
Outputs:
- hidden_out: bfloat16 [4096, 1536], P(('req', 'head'))
- states_out: bfloat16 [1024, 48, 64, 128], P('req', 'head')
- edge_inner_out: bfloat16 [1024, 3, 3072], P('req', None, 'head')
- edge_shared_out: bfloat16 [1024, 3, 256], P('req')
Inputs may be any that keep to these rules, and one draw needn't show every extreme that they name: counts: each slot's token rows are r * 4 to r * 4 + 3 of tokens; the first counts[r] of them are real. mig_ids: distinct old slots listed by owner: entry i is one of the slots i * 32 to (i + 1) * 32 - 1, those held by index i of req. mig_dest: a reordering of the slots in mig_ids. reorder: a permutation of all slots. The 32 new slots j with j // 32 = d take at most 1 values reorder[j] of any one block of 32 slots, and exactly 1 of some block.
All inputs are finite; a program needn't handle non-finite values.
Results may differ from a plain program's by a relative error of at most 0.013.
Values may be sent and summed in bfloat16 or wider, within the bound.
A program may use at most 128 MiB of HBM per device.

v0:
```python
import jax
import jax.numpy as jnp
from jax import lax
from jax.sharding import PartitionSpec as P

EPS = 1e-05
HIGH = lax.Precision.HIGHEST


def depthwise(edge, fresh, weight, offset_bias):
    sequence = jnp.concatenate([edge, fresh], axis=1).astype(jnp.float32)
    window = fresh.shape[1]
    summed = sequence[:, 0:window] * weight[0]
    for offset in range(1, weight.shape[0]):
        summed = summed + sequence[:, offset : offset + window] * weight[offset]
    return jax.nn.silu(summed + offset_bias)


def new_edge(edge, fresh, counts):
    sequence = jnp.concatenate([edge, fresh], axis=1)
    keep_rows = edge.shape[1]
    result = edge
    for length in range(1, fresh.shape[1] + 1):
        result = jnp.where(
            (counts == length)[:, None, None], sequence[:, length : length + keep_rows], result
        )
    return result


def rank_rows(partner, position, capacity):
    matching = partner[:, None] == partner[None, :]
    earlier = position[None, :] < position[:, None]
    ranking = jnp.sum(jnp.logical_and(matching, earlier), axis=1)
    return partner * capacity + ranking


def route_rows(anchor, first_slot, slot_count, all_slots, capacity):
    inverse = jnp.zeros(all_slots.shape, jnp.int32).at[anchor].set(all_slots)
    targets = lax.dynamic_slice_in_dim(inverse, first_slot, slot_count)
    send_rows = rank_rows(targets // slot_count, targets % slot_count, capacity)
    sources = lax.dynamic_slice_in_dim(anchor, first_slot, slot_count)
    recv_rows = rank_rows(sources // slot_count, jnp.arange(slot_count, dtype=jnp.int32), capacity)
    return (send_rows, recv_rows)


def migrate(item, mig_dest, slot_count, groups, device):
    length = item.shape[0]
    piece = -(-length // groups)
    padded = jnp.pad(item, (0, piece * groups - length)).reshape(groups, piece)
    first = lax.all_to_all(padded, "req", 0, 0, tiled=True)
    dest_dev = mig_dest // slot_count
    order = jnp.zeros((groups,), jnp.int32).at[dest_dev].set(jnp.arange(groups, dtype=jnp.int32))
    second = lax.all_to_all(first[order], "req", 0, 0, tiled=True)
    arrived = second.reshape(-1)[:length]
    target_local = mig_dest[order[device]] - device * slot_count
    return (arrived, target_local)


def local(
    tokens,
    pre_gain,
    inner_weight,
    shared_weight,
    conv_inner,
    conv_inner_bias,
    conv_shared,
    conv_shared_bias,
    step_bias,
    decay_log,
    skip_gain,
    gate_gain,
    out_weight,
    states,
    edge_inner,
    edge_shared,
    counts,
    mig_ids,
    mig_dest,
    reorder,
):
    slot_count, heads_here, head_dim, state_dim = states.shape
    inner_here = heads_here * head_dim
    lanes = state_dim
    groups = lax.axis_size("req")
    device = lax.axis_index("req")
    first_slot = device * slot_count
    stride = (slot_count + groups - 1) // groups
    all_slots = jnp.arange(slot_count * groups, dtype=jnp.int32)
    rows_in = tokens.astype(jnp.float32)
    normed = (
        rows_in * lax.rsqrt(jnp.mean(rows_in * rows_in, axis=-1, keepdims=True) + EPS) * pre_gain
    ).astype(jnp.bfloat16)
    inner_flat = inner_weight.reshape(inner_weight.shape[0], 2 * inner_here)
    piece_rows = lax.all_gather(normed, "head", axis=0, tiled=True)
    inner_rows = jnp.dot(piece_rows, inner_flat, preferred_element_type=jnp.float32).astype(
        jnp.bfloat16
    )
    shared_rows = jnp.dot(piece_rows, shared_weight, preferred_element_type=jnp.float32).astype(
        jnp.bfloat16
    )
    state_rows = heads_here * head_dim * state_dim // lanes
    inner_edge_rows = edge_inner.shape[1] * edge_inner.shape[2] // lanes
    shared_edge_rows = edge_shared.shape[1] * edge_shared.shape[2] // lanes
    packed = jnp.concatenate(
        [
            states.reshape(slot_count, state_rows, lanes),
            edge_inner.reshape(slot_count, inner_edge_rows, lanes),
            edge_shared.reshape(slot_count, shared_edge_rows, lanes),
        ],
        axis=1,
    )
    row_total = packed.shape[1]
    moving = mig_ids.shape[0] // groups
    own_id = mig_ids[device * moving]
    mig_local = own_id - first_slot
    item = lax.dynamic_index_in_dim(packed, mig_local, 0, keepdims=False).reshape(-1)
    arrived, target_local = migrate(item, mig_dest, slot_count, groups, device)
    arrived = arrived.reshape(row_total, lanes)
    send_rows, recv_rows = route_rows(reorder, first_slot, slot_count, all_slots, stride)
    buffer_rows = groups * stride
    send_idx = (
        jnp.zeros((buffer_rows,), jnp.int32)
        .at[send_rows]
        .set(jnp.arange(slot_count, dtype=jnp.int32))
    )
    send_buf = jnp.where((send_idx == target_local)[:, None, None], arrived[None], packed[send_idx])
    received = lax.all_to_all(send_buf, "req", 0, 0, tiled=True)
    moved = received[recv_rows]
    moved_states = moved[:, :state_rows].reshape(slot_count, heads_here, head_dim, state_dim)
    moved_inner = moved[:, state_rows : state_rows + inner_edge_rows].reshape(edge_inner.shape)
    moved_shared = moved[:, state_rows + inner_edge_rows :].reshape(edge_shared.shape)
    window = inner_rows.shape[0] // slot_count
    inner_rows = inner_rows.reshape(slot_count, window, 2 * inner_here)
    shared_rows = shared_rows.reshape(slot_count, window, shared_rows.shape[1])
    gate_part = inner_rows[:, :, :inner_here]
    value_part = inner_rows[:, :, inner_here:]
    fresh_shared = shared_rows[:, :, : 2 * state_dim]
    head_index = lax.axis_index("head")
    step_raw = lax.dynamic_slice_in_dim(
        shared_rows[:, :, 2 * state_dim :], head_index * heads_here, heads_here, axis=2
    )
    edge_inner_out = new_edge(moved_inner, value_part, counts)
    edge_shared_out = new_edge(moved_shared, fresh_shared, counts)
    mixed_inner = depthwise(moved_inner, value_part, conv_inner, conv_inner_bias)
    mixed_shared = depthwise(moved_shared, fresh_shared, conv_shared, conv_shared_bias)
    valid = jnp.arange(window)[None, :] < counts[:, None]
    step_size = jax.nn.softplus(step_raw.astype(jnp.float32) + step_bias)
    step_size = jnp.where(valid[:, :, None], step_size, 0.0)
    decay = -jnp.exp(decay_log)
    inputs = mixed_inner.reshape(slot_count, window, heads_here, head_dim)
    entries = mixed_shared[:, :, :state_dim]
    readouts = mixed_shared[:, :, state_dim:]
    factor = jnp.exp(step_size * decay)
    cum = [factor[:, 0]]
    for t in range(1, window):
        cum.append(cum[-1] * factor[:, t])
    cumulative = jnp.stack(cum, axis=1)
    span = {}
    for t in range(window):
        span[t, t] = jnp.ones_like(factor[:, 0])
        for s in range(t - 1, -1, -1):
            span[t, s] = span[t, s + 1] * factor[:, s + 1]
    held = moved_states.astype(jnp.float32)
    from_state = jnp.einsum("rhpn,rtn->rthp", held, readouts, precision=HIGH)
    overlap = jnp.einsum("rtn,rsn->rts", readouts, entries, precision=HIGH)
    weighted = step_size[:, :, :, None] * inputs
    produced = []
    for t in range(window):
        acc = cumulative[:, t, :, None] * from_state[:, t]
        for s in range(t + 1):
            coef = span[t, s] * overlap[:, t, s, None]
            acc = acc + coef[:, :, None] * weighted[:, s]
        produced.append(acc + skip_gain[None, :, None] * inputs[:, t])
    outputs = jnp.stack(produced, axis=1)
    last = window - 1
    pushed = jnp.stack([span[last, s] for s in range(window)], axis=1)[:, :, :, None] * weighted
    update = jnp.einsum("rshp,rsn->rhpn", pushed, entries, precision=HIGH)
    final = cumulative[:, last, :, None, None] * held + update
    states_out = final.astype(jnp.bfloat16)
    outputs = outputs.reshape(slot_count, window, inner_here)
    gated = outputs * jax.nn.silu(gate_part.astype(jnp.float32))
    square_part = jnp.sum(gated * gated, axis=-1).reshape(slot_count * window, 1)
    pre_scaled = (
        jnp.where(valid[:, :, None], gated * gate_gain, 0.0)
        .astype(jnp.bfloat16)
        .reshape(slot_count * window, inner_here)
    )
    partial = jnp.dot(pre_scaled, out_weight, preferred_element_type=jnp.float32)
    extra = jnp.broadcast_to(square_part, (partial.shape[0], 128))
    combined = jnp.concatenate([partial, extra], axis=1)
    reduced = lax.psum_scatter(combined, "head", scatter_dimension=0, tiled=True)
    full_inner = inner_here * lax.axis_size("head")
    scale = lax.rsqrt(reduced[:, -1:] / full_inner + EPS)
    hidden_out = (rows_in + reduced[:, : partial.shape[1]] * scale).astype(jnp.bfloat16)
    return (hidden_out, states_out, edge_inner_out, edge_shared_out)


def solution(mesh):
    placed = (
        P(("req", "head"), None),
        P(),
        P(None, None, "head"),
        P(),
        P(None, "head"),
        P("head"),
        P(),
        P(),
        P("head"),
        P("head"),
        P("head"),
        P("head"),
        P("head", None),
        P("req", "head", None, None),
        P("req", None, "head"),
        P("req", None, None),
        P("req"),
        P(),
        P(),
        P(),
    )
    return jax.shard_map(
        local,
        mesh=mesh,
        in_specs=placed,
        out_specs=(
            P(("req", "head"), None),
            P("req", "head", None, None),
            P("req", None, "head"),
            P("req", None, None),
        ),
        check_vma=False,
    )
```

profile of v0, /device:TPU:6, one launch (start us, length us, event | category | flops | bytes accessed | tf_op | source)
XLA Modules:
  0.0 188.7 jit_solution(13441082247929192009)
XLA Ops:
  7.2 1.3 dynamic_slice.26
  9.2 0.8 copy.235
  10.1 0.9 copy.234
  11.1 2.3 %pad_maximum_fusion = bf16[32,399,128]{2,1,0:T(8,128)(2,1)S(1)} fusion(bf16[32,6,128]{2,1,0:T(8,128)(2,1)S(1)} %reshape.332, bf16[32,9,128]{2,1,0:T(8,128)(2,1)S(1)} %reshape.331, bf16[32,384,128]{2,1,0:T(8,128)(2,1)} %bitcast.73), kind=kLoop, calls=%fused_computation.7 | loop fusion | flops 9805824 | bytes 6537216 | tf_op jit(solution)/shard_map/concatenate | solution.py:104
  13.4 1.7 copy-done.1
  15.8 1.3 reduce.39
  17.1 0.8 reshape.423
  17.9 7.6 %all-to-all-start = ((bf16[32,2,798]{2,1,0:T(2,128)(2,1)}), bf16[32,2,798]{2,1,0:T(2,128)(2,1)S(1)}, u32[]{:S(2)}, u32[]{:S(2)}) async-start(bf16[32,2,798]{2,1,0:T(2,128)(2,1)} %reshape.423), calls=%async_computation | async-start | bytes 229376 | tf_op jit(solution)/shard_map/all_to_all | solution.py:50
  25.5 4.3 %scatter_custom_fusion = s32[1024]{0:T(1024)S(1)} fusion(s32[1024]{0:T(1024)S(1)} %compare_select_fusion.1, s32[1024]{0:T(1024)S(1)} %iota.23, s32[]{:T(128)} %constant.75.clone.1), kind=kCustom, calls=%fused_computation.145 | custom fusion | bytes 4100 | tf_op jit(solution)/shard_map/scatter | solution.py:38
  30.2 0.7 scatter_custom_fusion.1
  30.9 0.7 scatter_custom_fusion.2
  35.8 0.7 gather_fusion
  36.4 0.7 reduce.40
  37.1 0.8 reshape.425
  37.9 7.4 %all-to-all-start.1 = ((bf16[32,2,798]{2,1,0:T(2,128)(2,1)}), bf16[32,2,798]{2,1,0:T(2,128)(2,1)S(1)}, u32[]{:S(2)}, u32[]{:S(2)}) async-start(bf16[32,2,798]{2,1,0:T(2,128)(2,1)} %reshape.425), calls=%async_computation.1 | async-start | bytes 229376 | tf_op jit(solution)/shard_map/all_to_all | solution.py:53
  45.3 4.6 %gather_fusion.1 = bf16[32,399,128]{2,1,0:T(8,128)(2,1)} fusion(bf16[32,399,128]{2,1,0:T(8,128)(2,1)} %copy-done.1, s32[1024]{0:T(1024)S(1)} %pad_clamp_fusion.1), kind=kCustom, calls=%fused_computation.1 | custom fusion | bytes 6537344 | tf_op jit(solution)/shard_map/gather | solution.py:126
  49.9 1.3 all-to-all-done.1
  51.4 0.6 reduce
  52.3 3.9 %broadcast_select_fusion = bf16[32,399,128]{2,1,0:T(8,128)(2,1)} fusion(bf16[32,399,128]{2,1,0:T(8,128)(2,1)} %gather_fusion.1, pred[32]{0:T(512)(128)(4,1)S(1)} %broadcast_compare_fusion.3, bf16[399,128]{1,0:T(8,128)(2,1)S(1)} %broadcast_in_dim.162), kind=kLoop, calls=%fused_computation.8 | loop fusion | flops 1634304 | bytes 6639392 | tf_op jit(solution)/shard_map/jit(_where)/select_n | solution.py:126
  56.2 6.5 %all-to-all-start.2 = ((bf16[32,399,128]{2,1,0:T(8,128)(2,1)}), bf16[32,399,128]{2,1,0:T(8,128)(2,1)}, u32[]{:S(2)}, u32[]{:S(2)}) async-start(bf16[32,399,128]{2,1,0:T(8,128)(2,1)} %broadcast_select_fusion), calls=%async_computation.2 | async-start | bytes 6553600 | tf_op jit(solution)/shard_map/all_to_all | solution.py:127
  62.9 28.9 %all_gather.3 = bf16[128,1536]{1,0:T(8,128)(2,1)S(1)} all-gather(bf16[16,1536]{1,0:T(8,128)(2,1)S(1)} %fusion.17), channel_id=1, replica_groups=mesh['req'=32,'head'=8] {'head'}, dimensions={0}, use_global_device_ids=true | all-gather | bytes 442368 | tf_op jit(solution)/shard_map/all_gather | solution.py:94
  92.5 2.2 %copy.278 = bf16[192,8,2,384]{3,1,2,0:T(8,128)(2,1)S(1)} copy(bf16[192,8,2,384]{3,2,1,0:T(2,128)(2,1)} %bitcast.74) | data formatting | bytes 4718592
  95.5 0.8 copy.238
  96.9 0.7 copy.277
  98.1 0.7 fusion.71
  98.8 3.4 %all-to-all-done.2 = bf16[32,399,128]{2,1,0:T(8,128)(2,1)} async-done(((bf16[32,399,128]{2,1,0:T(8,128)(2,1)}), bf16[32,399,128]{2,1,0:T(8,128)(2,1)}, u32[]{:S(2)}, u32[]{:S(2)}) %all-to-all-start.2) | async-done | bytes 3268640 | tf_op jit(solution)/shard_map/all_to_all | solution.py:127
  102.2 4.6 %gather_fusion.2 = bf16[32,399,128]{2,1,0:T(8,128)(2,1)} fusion(bf16[32,399,128]{2,1,0:T(8,128)(2,1)} %all-to-all-done.2, s32[1024]{0:T(1024)S(1)} %pad_clamp_fusion), kind=kCustom, calls=%fused_computation.2 | custom fusion | bytes 6537344 | tf_op jit(solution)/shard_map/gather | solution.py:128
  106.8 4.0 %slice.275 = bf16[32,384,128]{2,1,0:T(8,128)(2,1)} slice(bf16[32,399,128]{2,1,0:T(8,128)(2,1)} %gather_fusion.2), slice={[0:32], [0:384], [0:128]} | slice | bytes 6291456 | tf_op jit(solution)/shard_map/slice | solution.py:129
  112.0 9.3 %fusion.45 = f32[32,4,6,64]{3,1,2,0:T(4,128)S(1)} fusion(bf16[32,6,64,128]{3,2,1,0:T(8,128)(2,1)} %bitcast.69, f32[32,4,256]{2,1,0:T(4,128)S(1)} %divide_multiply_fusion.1), kind=kOutput, calls=%fused_computation.93 | convolution fusion | flops 75497472 | bytes 3407872 | tf_op jit(solution)/shard_map/rhpn,rtn->rthp/dot_general | solution.py:164
  121.3 1.6 slice_reduce_fusion.9
  123.5 0.7 copy.253
  124.2 0.7 copy.252
  124.9 0.7 copy.251
  125.6 0.7 copy.250
  126.3 1.3 broadcast_multiply_fusion
  127.5 2.9 %fusion.32 = (f32[32,6,64]{2,1,0:T(8,128)S(1)}, f32[32,6,64]{2,1,0:T(8,128)S(1)}) fusion(f32[32,4,6,64]{3,1,2,0:T(4,128)S(1)} %get-tuple-element.62, f32[32,4,6,64]{3,1,2,0:T(4,128)S(1)} %fusion.45, f32[32]{0:T(128)} %get-tuple-element.40, f32[32,6]{1,0:T(8,128)} %bitcast.76, f32[6]{0:T(128)} %param.30, f32[32,4,6,64]{3,1,2,0:T(4,128)S(1)} %get-tuple-element.61, ...), kind=kLoop, calls=%fused_computation.79 | loop fusion | flops 196608 | bytes 495640 | tf_op jit(solution)/shard_map/add | solution.py:173
  130.5 0.8 copy.244
  131.3 0.8 copy.243
  132.0 0.8 copy.248
  132.8 0.8 copy.247
  133.6 2.4 %fusion.31 = (f32[32,6,64]{2,1,0:T(8,128)S(1)}, f32[32,6,64]{2,1,0:T(8,128)S(1)}) fusion(f32[32,4,6,64]{3,1,2,0:T(4,128)S(1)} %get-tuple-element.62, f32[32,4,6,64]{3,1,2,0:T(4,128)S(1)} %fusion.45, f32[32]{0:T(128)} %get-tuple-element.48, f32[32,6]{1,0:T(8,128)S(1)} %copy.244, f32[32,6]{1,0:T(8,128)S(1)} %copy.243, f32[6]{0:T(128)} %param.30, ...), kind=kLoop, calls=%fused_computation.78 | loop fusion | flops 196608 | bytes 446488 | tf_op jit(solution)/shard_map/add | solution.py:173
  136.3 1.0 select_convert_fusion
  138.2 1.0 pad_maximum_fusion.1
  140.5 0.7 fusion.37
  141.2 13.4 %add_convert_fusion = bf16[32,6,64,128]{3,2,1,0:T(8,128)(2,1)} fusion(bf16[32,6,64,128]{3,2,1,0:T(8,128)(2,1)} %bitcast.70, f32[32,6]{1,0:T(8,128)S(1)} %copy-done.10, f32[32,4,6,64]{3,1,2,0:T(4,128)S(1)} %get-tuple-element.61, f32[32,4,6]{1,2,0:T(8,128)S(1)} %copy.259, f32[32,4,256]{2,1,0:T(4,128)S(1)} %divide_multiply_fusion.1), kind=kOutput, calls=%fused_computation.6 | convolution fusion | flops 81838080 | bytes 6897664 | tf_op jit(solution)/shard_map/rshp,rsn->rhpn/dot_general | solution.py:177
  154.6 24.7 %reduce-scatter.2.cloned.1.call-done = f32[16,1664]{1,0:T(8,128)} async-done(((f32[128,1664]{1,0:T(8,128)}), f32[16,1664]{1,0:T(8,128)}) %reduce-scatter.2.cloned.1.call-update) | async-done | bytes 106512 | tf_op jit(solution)/shard_map/reduce_scatter | solution.py:191
  179.3 0.9 fusion.56
  180.2 1.6 fusion.18
  (131 shorter events, 10.0 us)
Async XLA Ops:
  7.2 130.6 %copy-start = (bf16[384,1536]{1,0:T(8,128)(2,1)S(1)}, bf16[384,1536]{1,0:T(8,128)(2,1)}, u32[]{:S(2)}) copy-start(bf16[384,1536]{1,0:T(8,128)(2,1)} %param.32) | copy-start | bytes 3538948
  11.1 14.4 %copy-start.15 = (s32[1024]{0:T(1024)S(1)}, s32[1024]{0:T(1024)}, u32[]{:S(2)}) copy-start(s32[1024]{0:T(1024)} %param.39) | copy-start | bytes 12292
  11.1 19.8 %copy-start.23 = (s32[32]{0:T(128)S(1)}, s32[32]{0:T(128)}, u32[]{:S(2)}) copy-start(s32[32]{0:T(128)} %param.38) | copy-start | bytes 388
  11.1 22.4 %copy-start.8 = (bf16[16,1536]{1,0:T(8,128)(2,1)S(1)}, bf16[16,1536]{1,0:T(8,128)(2,1)}, u32[]{:S(2)}) copy-start(bf16[16,1536]{1,0:T(8,128)(2,1)} %param.20) | copy-start | bytes 147460
  13.4 1.7 copy-start.1
  17.9 17.7 %all-to-all-start = ((bf16[32,2,798]{2,1,0:T(2,128)(2,1)}), bf16[32,2,798]{2,1,0:T(2,128)(2,1)S(1)}, u32[]{:S(2)}, u32[]{:S(2)}) async-start(bf16[32,2,798]{2,1,0:T(2,128)(2,1)} %reshape.423), calls=%async_computation | async-start | bytes 229376 | tf_op jit(solution)/shard_map/all_to_all | solution.py:50
  37.9 13.3 %all-to-all-start.1 = ((bf16[32,2,798]{2,1,0:T(2,128)(2,1)}), bf16[32,2,798]{2,1,0:T(2,128)(2,1)S(1)}, u32[]{:S(2)}, u32[]{:S(2)}) async-start(bf16[32,2,798]{2,1,0:T(2,128)(2,1)} %reshape.425), calls=%async_computation.1 | async-start | bytes 229376 | tf_op jit(solution)/shard_map/all_to_all | solution.py:53
  56.2 6.6 %copy-start.13 = (f32[1536]{0:T(1024)S(1)}, f32[1536]{0:T(1024)}, u32[]{:S(2)}) copy-start(f32[1536]{0:T(1024)} %param.21) | copy-start | bytes 18436
  56.2 35.6 %copy-start.3 = (bf16[1536,304]{0,1:T(8,128)(2,1)S(1)}, bf16[1536,304]{0,1:T(8,128)(2,1)}, u32[]{:S(2)}) copy-start(bf16[1536,304]{0,1:T(8,128)(2,1)} %param.23) | copy-start | bytes 2801668
  56.2 45.9 %all-to-all-start.2 = ((bf16[32,399,128]{2,1,0:T(8,128)(2,1)}), bf16[32,399,128]{2,1,0:T(8,128)(2,1)}, u32[]{:S(2)}, u32[]{:S(2)}) async-start(bf16[32,399,128]{2,1,0:T(8,128)(2,1)} %broadcast_select_fusion), calls=%async_computation.2 | async-start | bytes 6553600 | tf_op jit(solution)/shard_map/all_to_all | solution.py:127
  62.7 116.6 %reduce-scatter.2.cloned.1.call-start = ((), (), s32[]{:S(2)}) async-start(), calls=%async_computation.4 | async-start | bytes 958464 | tf_op jit(solution)/shard_map/reduce_scatter | solution.py:191
  92.4 3.0 %copy-start.21 = (s32[32]{0:T(128)S(1)}, s32[32]{0:T(128)}, u32[]{:S(2)}) copy-start(s32[32]{0:T(128)} %param.36) | copy-start | bytes 388
  92.4 3.0 %copy-start.24 = (f32[6]{0:T(128)S(1)}, f32[6]{0:T(128)}, u32[]{:S(2)}) copy-start(f32[6]{0:T(128)} %param.29) | copy-start | bytes 76
  92.4 3.0 %copy-start.20 = (f32[6]{0:T(128)S(1)}, f32[6]{0:T(128)}, u32[]{:S(2)}) copy-start(f32[6]{0:T(128)} %param.28) | copy-start | bytes 76
  92.4 5.5 %copy-start.14 = (f32[4,384]{1,0:T(4,128)S(1)}, f32[4,384]{1,0:T(4,128)}, u32[]{:S(2)}) copy-start(f32[4,384]{1,0:T(4,128)} %param.24) | copy-start | bytes 18436
  92.5 5.6 %copy-start.16 = (f32[4,256]{1,0:T(4,128)S(1)}, f32[4,256]{1,0:T(4,128)}, u32[]{:S(2)}) copy-start(f32[4,256]{1,0:T(4,128)} %param.26) | copy-start | bytes 12292
  95.4 11.4 %copy-start.18 = (pred[32,4]{0,1:T(4,128)(4,1)}, pred[32,4]{0,1:T(4,128)(4,1)S(1)}, u32[]{:S(2)}) copy-start(pred[32,4]{0,1:T(4,128)(4,1)S(1)} %iota_compare_fusion.1) | copy-start | bytes 388
  106.8 4.1 %copy-start.2 = (bf16[32,399,128]{2,1,0:T(8,128)(2,1)S(1)}, bf16[32,399,128]{2,1,0:T(8,128)(2,1)}, u32[]{:S(2)}) copy-start(bf16[32,399,128]{2,1,0:T(8,128)(2,1)} %gather_fusion.2) | copy-start | bytes 9805828
  106.8 4.1 %slice-start = ((bf16[32,399,128]{2,1,0:T(8,128)(2,1)}), bf16[32,9,128]{2,1,0:T(8,128)(2,1)S(1)}, s32[]{:S(2)}) async-start(bf16[32,399,128]{2,1,0:T(8,128)(2,1)} %gather_fusion.2), calls=%async_computation.5 | async-start | bytes 262144 | tf_op jit(solution)/shard_map/slice | solution.py:130
  106.8 4.3 %copy-start.17 = (f32[384]{0:T(512)S(1)}, f32[384]{0:T(512)}, u32[]{:S(2)}) copy-start(f32[384]{0:T(512)} %param.25) | copy-start | bytes 4612
  110.8 0.7 copy-start.19
  110.9 10.4 %copy-start.4 = (bf16[32,3,384]{2,1,0:T(4,128)(2,1)}, bf16[32,3,384]{2,1,0:T(4,128)(2,1)S(1)}, u32[]{:S(2)}) copy-start(bf16[32,3,384]{2,1,0:T(4,128)(2,1)S(1)} %reshape.335) | copy-start | bytes 221188
  111.3 14.3 %copy-start.6 = (bf16[32,3,256]{2,1,0:T(4,128)(2,1)}, bf16[32,3,256]{2,1,0:T(4,128)(2,1)S(1)}, u32[]{:S(2)}) copy-start(bf16[32,3,256]{2,1,0:T(4,128)(2,1)S(1)} %reshape.333) | copy-start | bytes 147460
  136.0 3.3 %copy-start.11 = (f32[32,1,6]{0,1,2:T(1,128)S(1)}, f32[32,1,6]{0,1,2:T(1,128)}, u32[]{:S(2)}) copy-start(f32[32,1,6]{0,1,2:T(1,128)} %get-tuple-element.54) | copy-start | bytes 2308
  136.0 3.3 %copy-start.12 = (f32[32,1,6]{0,1,2:T(1,128)S(1)}, f32[32,1,6]{0,1,2:T(1,128)}, u32[]{:S(2)}) copy-start(f32[32,1,6]{0,1,2:T(1,128)} %get-tuple-element.55) | copy-start | bytes 2308
  136.0 3.5 %copy-start.22 = (s32[32]{0:T(128)S(1)}, s32[32]{0:T(128)}, u32[]{:S(2)}) copy-start(s32[32]{0:T(128)} %param.36) | copy-start | bytes 388
  136.3 3.3 %copy-start.7 = (bf16[32,3,256]{2,1,0:T(4,128)(2,1)S(1)}, bf16[32,3,256]{2,1,0:T(4,128)(2,1)}, u32[]{:S(2)}) copy-start(bf16[32,3,256]{2,1,0:T(4,128)(2,1)} %copy-done.6) | copy-start | bytes 147460
  137.3 3.2 %copy-start.5 = (bf16[32,3,384]{2,1,0:T(4,128)(2,1)S(1)}, bf16[32,3,384]{2,1,0:T(4,128)(2,1)}, u32[]{:S(2)}) copy-start(bf16[32,3,384]{2,1,0:T(4,128)(2,1)} %copy-done.4) | copy-start | bytes 221188
  137.6 3.6 %copy-start.10 = (f32[32,6]{1,0:T(8,128)S(1)}, f32[32,6]{1,0:T(8,128)}, u32[]{:S(2)}) copy-start(f32[32,6]{1,0:T(8,128)} %copy.250) | copy-start | bytes 2308
  141.2 39.0 %copy-start.9 = (bf16[16,1536]{1,0:T(8,128)(2,1)S(1)}, bf16[16,1536]{1,0:T(8,128)(2,1)}, u32[]{:S(2)}) copy-start(bf16[16,1536]{1,0:T(8,128)(2,1)} %param.20) | copy-start | bytes 147460
Sparse Core Ops, SparseCore 0:
  139.3 39.9 reduce-scatter.1
where the time goes:
time: 190 us; the launch traced here: 189 us
  local copies, waits for them, and re-layouts  42.9 us (23%)
  waiting for transfers between devices  29.5 us (16%)
  blocking collectives  28.9 us (15%)
  matrix products  24.2 us (13%)
  other arithmetic  23.6 us (12%)
  starting transfers between devices  21.5 us (11%)
  between operations  18 us (9%)
    all_gather x1, blocking collectives, local(): piece_rows = lax.all_gather(normed, 'head', axis=0, tiled=True)  28.9 us
    reduce_scatter x1, waiting for transfers between devices, local(): lax.psum_scatter(combined, 'head', scatter_dimension=0, tiled=True)  24.7 us
    dot_general x1, matrix products, local(): update = jnp.einsum('rshp,rsn->rhpn', pushed, entries, precision=HIGH)  13.4 us
    dot_general x1, matrix products, local(): from_state = jnp.einsum('rhpn,rtn->rthp', held, readouts, precision=HIGH)  9.26 us
    unnamed x61, local copies, waits for them, and re-layouts  8.57 us
    all_to_all x1, starting transfers between devices, migrate(): first = lax.all_to_all(padded, 'req', 0, 0, tiled=True)  7.56 us
    all_to_all x1, starting transfers between devices, migrate(): second = lax.all_to_all(first[order], 'req', 0, 0, tiled=True)  7.38 us
    all_to_all x1, starting transfers between devices, local(): received = lax.all_to_all(send_buf, 'req', 0, 0, tiled=True)  6.51 us
  transfers between devices with their start and end apart: 4, of which 3 were waited for; matrix products, arithmetic and copies ran while one was open for 18% of the time, Pallas kernels for 0%

commit v1 on v0

--- a/solution.py
+++ b/solution.py
@@ -91,7 +91,11 @@
         rows_in * lax.rsqrt(jnp.mean(rows_in * rows_in, axis=-1, keepdims=True) + EPS) * pre_gain
     ).astype(jnp.bfloat16)
     inner_flat = inner_weight.reshape(inner_weight.shape[0], 2 * inner_here)
-    piece_rows = lax.all_gather(normed, "head", axis=0, tiled=True)
+    size = lax.axis_size("head")
+    repeats = [size if d == 0 else 1 for d in range(normed.ndim)]
+    piece_rows = lax.all_to_all(
+        jnp.tile(normed, repeats), "head", split_axis=0, concat_axis=0, tiled=True
+    )
     inner_rows = jnp.dot(piece_rows, inner_flat, preferred_element_type=jnp.float32).astype(
         jnp.bfloat16
     )

time: 190 us -> 202 us (1.063)
  blocking collectives: 28.9 us -> 0 us
  waiting for transfers between devices: 29.5 us -> 44.1 us
  local copies, waits for them, and re-layouts: 42.9 us -> 54 us
  starting transfers between devices: 21.5 us -> 30 us
  matrix products: 24.2 us -> 27.8 us
  other arithmetic: 23.6 us -> 26.2 us
    all_gather x1 -> x0, blocking collectives: 28.9 us -> none  [local(): piece_rows = lax.all_gather(normed, 'head', axis=0, tiled=True)]
    all_to_all x1, waiting for transfers between devices: 3.41 us -> 16.7 us  [local(): received = lax.all_to_all(send_buf, 'req', 0, 0, tiled=True)]
    all_to_all x0 -> x1, starting transfers between devices: none -> 8.47 us  [local(): lax.all_to_all(jnp.tile(normed, repeats), 'head', split_axis=0, concat_ax...]
    reduce_scatter x1, waiting for transfers between devices: 24.7 us -> 19.9 us  [local(): lax.psum_scatter(combined, 'head', scatter_dimension=0, tiled=True)]
    all_to_all x0 -> x1, waiting for transfers between devices: none -> 3.56 us  [local(): lax.all_to_all(jnp.tile(normed, repeats), 'head', split_axis=0, concat_ax...]
    all_to_all x1, waiting for transfers between devices: 1.33 us -> 3.97 us  [migrate(): second = lax.all_to_all(first[order], 'req', 0, 0, tiled=True)]
    unnamed x61 -> x67, local copies, waits for them, and re-layouts: 8.57 us -> 9.29 us
  transfers between devices with their start and end apart: 4 -> 5, of which waited for: 3 -> 4; matrix products, arithmetic and copies ran while one was open for 18% -> 27% of each run, Pallas kernels for 0% -> 0%
where the time goes in v1:
time: 202 us; the launch traced here: 200 us
  local copies, waits for them, and re-layouts  54 us (27%)
  waiting for transfers between devices  44.1 us (22%)
  starting transfers between devices  30 us (15%)
  matrix products  27.8 us (14%)
  other arithmetic  26.2 us (13%)
  between operations  17.9 us (9%)
    reduce_scatter x1, waiting for transfers between devices, local(): lax.psum_scatter(combined, 'head', scatter_dimension=0, tiled=True)  19.9 us
    all_to_all x1, waiting for transfers between devices, local(): received = lax.all_to_all(send_buf, 'req', 0, 0, tiled=True)  16.7 us
    dot_general x1, matrix products, local(): update = jnp.einsum('rshp,rsn->rhpn', pushed, entries, precision=HIGH)  13.4 us
    unnamed x67, local copies, waits for them, and re-layouts  9.29 us
    dot_general x1, matrix products, local(): from_state = jnp.einsum('rhpn,rtn->rthp', held, readouts, precision=HIGH)  9.26 us
    all_to_all x1, starting transfers between devices, local(): lax.all_to_all(jnp.tile(normed, repeats), 'head', split_axis=0, concat_ax...  8.47 us
    all_to_all x1, starting transfers between devices, migrate(): first = lax.all_to_all(padded, 'req', 0, 0, tiled=True)  7.56 us
    all_to_all x1, starting transfers between devices, migrate(): second = lax.all_to_all(first[order], 'req', 0, 0, tiled=True)  7.38 us
  transfers between devices with their start and end apart: 5, of which 4 were waited for; matrix products, arithmetic and copies ran while one was open for 27% of the time, Pallas kernels for 0%

profile of v1, /device:TPU:6, one launch (start us, length us, event | category | flops | bytes accessed | tf_op | source)
XLA Modules:
  0.0 200.1 jit_solution(9827122690681241946)
XLA Ops:
  7.2 1.3 dynamic_slice.26
  9.2 0.8 copy.235
  10.1 0.9 copy.234
  11.1 2.3 %pad_maximum_fusion = bf16[32,399,128]{2,1,0:T(8,128)(2,1)S(1)} fusion(bf16[32,6,128]{2,1,0:T(8,128)(2,1)S(1)} %reshape.339, bf16[32,9,128]{2,1,0:T(8,128)(2,1)S(1)} %reshape.338, bf16[32,384,128]{2,1,0:T(8,128)(2,1)} %bitcast.76), kind=kLoop, calls=%fused_computation.7 | loop fusion | flops 9805824 | bytes 6537216 | tf_op jit(solution)/shard_map/concatenate | solution.py:108
  13.4 1.7 copy-done.1
  15.8 1.3 reduce.39
  17.1 0.8 reshape.430
  17.9 7.6 %all-to-all-start.1 = ((bf16[32,2,798]{2,1,0:T(2,128)(2,1)}), bf16[32,2,798]{2,1,0:T(2,128)(2,1)S(1)}, u32[]{:S(2)}, u32[]{:S(2)}) async-start(bf16[32,2,798]{2,1,0:T(2,128)(2,1)} %reshape.430), calls=%async_computation.1 | async-start | bytes 229376 | tf_op jit(solution)/shard_map/all_to_all | solution.py:50
  25.7 4.3 %scatter_custom_fusion = s32[1024]{0:T(1024)S(1)} fusion(s32[1024]{0:T(1024)S(1)} %compare_select_fusion.1, s32[1024]{0:T(1024)S(1)} %iota.23, s32[]{:T(128)} %constant.75.clone.1), kind=kCustom, calls=%fused_computation.145 | custom fusion | bytes 4100 | tf_op jit(solution)/shard_map/scatter | solution.py:38
  33.4 0.8 reshape.432
  34.2 7.4 %all-to-all-start.2 = ((bf16[32,2,798]{2,1,0:T(2,128)(2,1)}), bf16[32,2,798]{2,1,0:T(2,128)(2,1)S(1)}, u32[]{:S(2)}, u32[]{:S(2)}) async-start(bf16[32,2,798]{2,1,0:T(2,128)(2,1)} %reshape.432), calls=%async_computation.2 | async-start | bytes 229376 | tf_op jit(solution)/shard_map/all_to_all | solution.py:53
  43.5 4.0 %all-to-all-done.2 = bf16[32,2,798]{2,1,0:T(2,128)(2,1)S(1)} async-done(((bf16[32,2,798]{2,1,0:T(2,128)(2,1)}), bf16[32,2,798]{2,1,0:T(2,128)(2,1)S(1)}, u32[]{:S(2)}, u32[]{:S(2)}) %all-to-all-start.2) | async-done | bytes 102176 | tf_op jit(solution)/shard_map/all_to_all | solution.py:53
  47.5 0.8 tile.2
  48.3 8.5 %all-to-all-start = ((bf16[8,16,1536]{2,1,0:T(8,128)(2,1)}), bf16[8,16,1536]{2,1,0:T(8,128)(2,1)S(1)}, u32[]{:S(2)}, u32[]{:S(2)}) async-start(bf16[8,16,1536]{2,1,0:T(8,128)(2,1)} %tile.2), calls=%async_computation | async-start | bytes 786432 | tf_op jit(solution)/shard_map/all_to_all | solution.py:96
  56.8 4.6 %gather_fusion.1 = bf16[32,399,128]{2,1,0:T(8,128)(2,1)} fusion(bf16[32,399,128]{2,1,0:T(8,128)(2,1)} %copy-done.1, s32[1024]{0:T(1024)S(1)} %pad_clamp_fusion.1), kind=kCustom, calls=%fused_computation.1 | custom fusion | bytes 6537344 | tf_op jit(solution)/shard_map/gather | solution.py:130
  64.2 3.9 %broadcast_select_fusion = bf16[32,399,128]{2,1,0:T(8,128)(2,1)} fusion(bf16[32,399,128]{2,1,0:T(8,128)(2,1)} %gather_fusion.1, pred[32]{0:T(512)(128)(4,1)S(1)} %broadcast_compare_fusion.3, bf16[399,128]{1,0:T(8,128)(2,1)S(1)} %broadcast_in_dim.162), kind=kLoop, calls=%fused_computation.8 | loop fusion | flops 1634304 | bytes 6639392 | tf_op jit(solution)/shard_map/jit(_where)/select_n | solution.py:130
  68.1 3.6 %all-to-all-done = bf16[8,16,1536]{2,1,0:T(8,128)(2,1)S(1)} async-done(((bf16[8,16,1536]{2,1,0:T(8,128)(2,1)}), bf16[8,16,1536]{2,1,0:T(8,128)(2,1)S(1)}, u32[]{:S(2)}, u32[]{:S(2)}) %all-to-all-start) | async-done | bytes 393248 | tf_op jit(solution)/shard_map/all_to_all | solution.py:96
  72.4 6.4 %all-to-all-start.3 = ((bf16[32,399,128]{2,1,0:T(8,128)(2,1)}), bf16[32,399,128]{2,1,0:T(8,128)(2,1)}, u32[]{:S(2)}, u32[]{:S(2)}) async-start(bf16[32,399,128]{2,1,0:T(8,128)(2,1)} %broadcast_select_fusion), calls=%async_computation.3 | async-start | bytes 6553600 | tf_op jit(solution)/shard_map/all_to_all | solution.py:131
  79.1 2.1 %copy.278 = bf16[192,8,2,384]{3,1,2,0:T(8,128)(2,1)S(1)} copy(bf16[192,8,2,384]{3,2,1,0:T(2,128)(2,1)} %bitcast.77) | data formatting | bytes 4718592
  84.2 1.4 fusion.72
  85.6 2.3 %convolution_convert_fusion.1 = bf16[128,304]{0,1:T(8,128)(2,1)} fusion(bf16[128,1536]{1,0:T(8,128)(2,1)} %bitcast.74, bf16[1536,304]{0,1:T(8,128)(2,1)} %param.23), kind=kOutput, calls=%fused_computation.10 | convolution fusion | flops 119576576 | bytes 1404928 | tf_op jit(solution)/shard_map/dot_general | solution.py:102
  87.9 1.6 copy.230
  89.5 1.6 reshape.336
  91.1 1.4 slice.266
  92.5 1.5 slice.269
  94.0 2.1 %convolution_convert_fusion = bf16[128,768]{1,0:T(8,128)(2,1)} fusion(bf16[128,1536]{1,0:T(8,128)(2,1)} %bitcast.75, bf16[1536,768]{1,0:T(8,128)(2,1)S(1)} %bitcast.72), kind=kOutput, calls=%fused_computation.9 | convolution fusion | flops 302088192 | bytes 2949120 | tf_op jit(solution)/shard_map/dot_general | solution.py:99
  96.1 1.0 reshape.344
  97.1 0.8 constant_dynamic-slice_fusion.1
  98.1 0.8 multiply_exponential_fusion
  98.8 0.8 copy.238
  101.6 16.7 %all-to-all-done.3 = bf16[32,399,128]{2,1,0:T(8,128)(2,1)} async-done(((bf16[32,399,128]{2,1,0:T(8,128)(2,1)}), bf16[32,399,128]{2,1,0:T(8,128)(2,1)}, u32[]{:S(2)}, u32[]{:S(2)}) %all-to-all-start.3) | async-done | bytes 3268640 | tf_op jit(solution)/shard_map/all_to_all | solution.py:131
  118.3 4.7 %gather_fusion.2 = bf16[32,399,128]{2,1,0:T(8,128)(2,1)} fusion(bf16[32,399,128]{2,1,0:T(8,128)(2,1)} %all-to-all-done.3, s32[1024]{0:T(1024)} %pad_clamp_fusion), kind=kCustom, calls=%fused_computation.2 | custom fusion | bytes 6537344 | tf_op jit(solution)/shard_map/gather | solution.py:132
  123.0 4.0 %slice.275 = bf16[32,384,128]{2,1,0:T(8,128)(2,1)} slice(bf16[32,399,128]{2,1,0:T(8,128)(2,1)} %gather_fusion.2), slice={[0:32], [0:384], [0:128]} | slice | bytes 6291456 | tf_op jit(solution)/shard_map/slice | solution.py:133
  128.3 9.3 %fusion.45 = f32[32,4,6,64]{3,1,2,0:T(4,128)S(1)} fusion(bf16[32,6,64,128]{3,2,1,0:T(8,128)(2,1)} %bitcast.70, f32[32,4,256]{2,1,0:T(4,128)S(1)} %divide_multiply_fusion.1), kind=kOutput, calls=%fused_computation.93 | convolution fusion | flops 75497472 | bytes 3407872 | tf_op jit(solution)/shard_map/rhpn,rtn->rthp/dot_general | solution.py:168
  137.6 1.6 slice_reduce_fusion.9
  142.5 1.3 broadcast_multiply_fusion
  143.8 2.9 %fusion.32 = (f32[32,6,64]{2,1,0:T(8,128)S(1)}, f32[32,6,64]{2,1,0:T(8,128)S(1)}) fusion(f32[32,4,6,64]{3,1,2,0:T(4,128)S(1)} %get-tuple-element.62, f32[32,4,6,64]{3,1,2,0:T(4,128)S(1)} %fusion.45, f32[32]{0:T(128)} %get-tuple-element.40, f32[32,6]{1,0:T(8,128)} %bitcast.79, f32[6]{0:T(128)} %param.30, f32[32,4,6,64]{3,1,2,0:T(4,128)S(1)} %get-tuple-element.61, ...), kind=kLoop, calls=%fused_computation.79 | loop fusion | flops 196608 | bytes 495640 | tf_op jit(solution)/shard_map/add | solution.py:177
  146.8 0.8 copy.244
  147.5 0.8 copy.243
  148.3 0.8 copy.248
  149.0 0.8 copy.247
  149.9 2.4 %fusion.31 = (f32[32,6,64]{2,1,0:T(8,128)S(1)}, f32[32,6,64]{2,1,0:T(8,128)S(1)}) fusion(f32[32,4,6,64]{3,1,2,0:T(4,128)S(1)} %get-tuple-element.62, f32[32,4,6,64]{3,1,2,0:T(4,128)S(1)} %fusion.45, f32[32]{0:T(128)} %get-tuple-element.48, f32[32,6]{1,0:T(8,128)S(1)} %copy.244, f32[32,6]{1,0:T(8,128)S(1)} %copy.243, f32[6]{0:T(128)} %param.30, ...), kind=kLoop, calls=%fused_computation.78 | loop fusion | flops 196608 | bytes 446488 | tf_op jit(solution)/shard_map/add | solution.py:177
  152.5 1.0 select_convert_fusion
  154.4 1.0 pad_maximum_fusion.1
  157.5 13.4 %add_convert_fusion = bf16[32,6,64,128]{3,2,1,0:T(8,128)(2,1)} fusion(bf16[32,6,64,128]{3,2,1,0:T(8,128)(2,1)} %bitcast.71, f32[32,6]{1,0:T(8,128)S(1)} %copy-done.10, f32[32,4,6,64]{3,1,2,0:T(4,128)S(1)} %get-tuple-element.61, f32[32,4,6]{1,2,0:T(8,128)S(1)} %copy.259, f32[32,4,256]{2,1,0:T(4,128)S(1)} %divide_multiply_fusion.1), kind=kOutput, calls=%fused_computation.6 | convolution fusion | flops 81838080 | bytes 6897664 | tf_op jit(solution)/shard_map/rshp,rsn->rhpn/dot_general | solution.py:181
  170.9 19.9 %reduce-scatter.2.cloned.1.call-done = f32[16,1664]{1,0:T(8,128)} async-done(((f32[128,1664]{1,0:T(8,128)}), f32[16,1664]{1,0:T(8,128)}) %reduce-scatter.2.cloned.1.call-update) | async-done | bytes 106512 | tf_op jit(solution)/shard_map/reduce_scatter | solution.py:195
  190.7 0.9 fusion.56
  191.6 1.6 fusion.18
  (139 shorter events, 20.2 us)
Async XLA Ops:
  7.2 146.8 %copy-start = (bf16[384,1536]{1,0:T(8,128)(2,1)S(1)}, bf16[384,1536]{1,0:T(8,128)(2,1)}, u32[]{:S(2)}) copy-start(bf16[384,1536]{1,0:T(8,128)(2,1)} %param.32) | copy-start | bytes 3538948
  11.1 14.4 %copy-start.8 = (bf16[16,1536]{1,0:T(8,128)(2,1)S(1)}, bf16[16,1536]{1,0:T(8,128)(2,1)}, u32[]{:S(2)}) copy-start(bf16[16,1536]{1,0:T(8,128)(2,1)} %param.20) | copy-start | bytes 147460
  11.1 14.6 %copy-start.18 = (s32[1024]{0:T(1024)S(1)}, s32[1024]{0:T(1024)}, u32[]{:S(2)}) copy-start(s32[1024]{0:T(1024)} %param.39) | copy-start | bytes 12292
  11.1 19.9 %copy-start.27 = (s32[32]{0:T(128)S(1)}, s32[32]{0:T(128)}, u32[]{:S(2)}) copy-start(s32[32]{0:T(128)} %param.38) | copy-start | bytes 388
  13.4 1.7 copy-start.1
  15.1 26.4 %copy-start.16 = (f32[1536]{0:T(1024)S(1)}, f32[1536]{0:T(1024)}, u32[]{:S(2)}) copy-start(f32[1536]{0:T(1024)} %param.21) | copy-start | bytes 18436
  17.9 13.9 %all-to-all-start.1 = ((bf16[32,2,798]{2,1,0:T(2,128)(2,1)}), bf16[32,2,798]{2,1,0:T(2,128)(2,1)S(1)}, u32[]{:S(2)}, u32[]{:S(2)}) async-start(bf16[32,2,798]{2,1,0:T(2,128)(2,1)} %reshape.430), calls=%async_computation.1 | async-start | bytes 229376 | tf_op jit(solution)/shard_map/all_to_all | solution.py:50
  34.2 13.3 %all-to-all-start.2 = ((bf16[32,2,798]{2,1,0:T(2,128)(2,1)}), bf16[32,2,798]{2,1,0:T(2,128)(2,1)S(1)}, u32[]{:S(2)}, u32[]{:S(2)}) async-start(bf16[32,2,798]{2,1,0:T(2,128)(2,1)} %reshape.432), calls=%async_computation.2 | async-start | bytes 229376 | tf_op jit(solution)/shard_map/all_to_all | solution.py:53
  48.3 23.4 %all-to-all-start = ((bf16[8,16,1536]{2,1,0:T(8,128)(2,1)}), bf16[8,16,1536]{2,1,0:T(8,128)(2,1)S(1)}, u32[]{:S(2)}, u32[]{:S(2)}) async-start(bf16[8,16,1536]{2,1,0:T(8,128)(2,1)} %tile.2), calls=%async_computation | async-start | bytes 786432 | tf_op jit(solution)/shard_map/all_to_all | solution.py:96
  71.7 0.7 copy-start.3
  72.4 45.8 %all-to-all-start.3 = ((bf16[32,399,128]{2,1,0:T(8,128)(2,1)}), bf16[32,399,128]{2,1,0:T(8,128)(2,1)}, u32[]{:S(2)}, u32[]{:S(2)}) async-start(bf16[32,399,128]{2,1,0:T(8,128)(2,1)} %broadcast_select_fusion), calls=%async_computation.3 | async-start | bytes 6553600 | tf_op jit(solution)/shard_map/all_to_all | solution.py:131
  78.9 3.4 %copy-start.17 = (f32[4,384]{1,0:T(4,128)S(1)}, f32[4,384]{1,0:T(4,128)}, u32[]{:S(2)}) copy-start(f32[4,384]{1,0:T(4,128)} %param.24) | copy-start | bytes 18436
  78.9 111.9 %reduce-scatter.2.cloned.1.call-start = ((), (), s32[]{:S(2)}) async-start(), calls=%async_computation.5 | async-start | bytes 958464 | tf_op jit(solution)/shard_map/reduce_scatter | solution.py:195
  83.5 39.5 %copy-start.24 = (pred[32,4]{0,1:T(4,128)(4,1)}, pred[32,4]{0,1:T(4,128)(4,1)S(1)}, u32[]{:S(2)}) copy-start(pred[32,4]{0,1:T(4,128)(4,1)S(1)} %iota_compare_fusion.1) | copy-start | bytes 388
  123.0 4.1 %copy-start.2 = (bf16[32,399,128]{2,1,0:T(8,128)(2,1)S(1)}, bf16[32,399,128]{2,1,0:T(8,128)(2,1)}, u32[]{:S(2)}) copy-start(bf16[32,399,128]{2,1,0:T(8,128)(2,1)} %gather_fusion.2) | copy-start | bytes 9805828
  123.0 4.2 %slice-start = ((bf16[32,399,128]{2,1,0:T(8,128)(2,1)}), bf16[32,9,128]{2,1,0:T(8,128)(2,1)S(1)}, s32[]{:S(2)}) async-start(bf16[32,399,128]{2,1,0:T(8,128)(2,1)} %gather_fusion.2), calls=%async_computation.6 | async-start | bytes 262144 | tf_op jit(solution)/shard_map/slice | solution.py:134
  123.0 4.3 %copy-start.13 = (f32[384]{0:T(512)S(1)}, f32[384]{0:T(512)}, u32[]{:S(2)}) copy-start(f32[384]{0:T(512)} %get-tuple-element.51) | copy-start | bytes 4612
  123.0 4.3 %copy-start.14 = (f32[384]{0:T(512)S(1)}, f32[384]{0:T(512)}, u32[]{:S(2)}) copy-start(f32[384]{0:T(512)} %get-tuple-element.52) | copy-start | bytes 4612
  123.0 4.3 %copy-start.15 = (f32[384]{0:T(512)S(1)}, f32[384]{0:T(512)}, u32[]{:S(2)}) copy-start(f32[384]{0:T(512)} %get-tuple-element.53) | copy-start | bytes 4612
  123.0 4.3 %copy-start.23 = (f32[384]{0:T(512)S(1)}, f32[384]{0:T(512)}, u32[]{:S(2)}) copy-start(f32[384]{0:T(512)} %param.25) | copy-start | bytes 4612
  123.0 4.6 %copy-start.5 = (bf16[32,4,256]{2,1,0:T(4,128)(2,1)S(1)}, bf16[32,4,256]{2,1,0:T(4,128)(2,1)}, u32[]{:S(2)}) copy-start(bf16[32,4,256]{2,1,0:T(4,128)(2,1)} %slice.269) | copy-start | bytes 196612
  127.1 0.7 copy-start.19
  127.1 0.7 copy-start.20
  127.1 0.7 copy-start.21
  127.1 0.7 copy-start.22
  127.1 0.7 copy-start.25
  127.6 14.2 %copy-start.6 = (bf16[32,3,256]{2,1,0:T(4,128)(2,1)}, bf16[32,3,256]{2,1,0:T(4,128)(2,1)S(1)}, u32[]{:S(2)}) copy-start(bf16[32,3,256]{2,1,0:T(4,128)(2,1)S(1)} %reshape.340) | copy-start | bytes 147460
  152.3 3.3 %copy-start.26 = (s32[32]{0:T(128)S(1)}, s32[32]{0:T(128)}, u32[]{:S(2)}) copy-start(s32[32]{0:T(128)} %param.36) | copy-start | bytes 388
  152.3 3.3 %copy-start.11 = (f32[32,1,6]{0,1,2:T(1,128)S(1)}, f32[32,1,6]{0,1,2:T(1,128)}, u32[]{:S(2)}) copy-start(f32[32,1,6]{0,1,2:T(1,128)} %get-tuple-element.54) | copy-start | bytes 2308
  152.3 3.2 %copy-start.12 = (f32[32,1,6]{0,1,2:T(1,128)S(1)}, f32[32,1,6]{0,1,2:T(1,128)}, u32[]{:S(2)}) copy-start(f32[32,1,6]{0,1,2:T(1,128)} %get-tuple-element.55) | copy-start | bytes 2308
  152.5 3.3 %copy-start.4 = (bf16[32,4,304]{2,1,0:T(4,128)(2,1)S(1)}, bf16[32,4,304]{2,1,0:T(4,128)(2,1)}, u32[]{:S(2)}) copy-start(bf16[32,4,304]{2,1,0:T(4,128)(2,1)} %reshape.336) | copy-start | bytes 233476
  152.5 3.3 %copy-start.7 = (bf16[32,3,256]{2,1,0:T(4,128)(2,1)S(1)}, bf16[32,3,256]{2,1,0:T(4,128)(2,1)}, u32[]{:S(2)}) copy-start(bf16[32,3,256]{2,1,0:T(4,128)(2,1)} %copy-done.6) | copy-start | bytes 147460
  153.9 3.6 %copy-start.10 = (f32[32,6]{1,0:T(8,128)S(1)}, f32[32,6]{1,0:T(8,128)}, u32[]{:S(2)}) copy-start(f32[32,6]{1,0:T(8,128)} %copy.250) | copy-start | bytes 2308
  157.5 34.1 %copy-start.9 = (bf16[16,1536]{1,0:T(8,128)(2,1)S(1)}, bf16[16,1536]{1,0:T(8,128)(2,1)}, u32[]{:S(2)}) copy-start(bf16[16,1536]{1,0:T(8,128)(2,1)} %param.20) | copy-start | bytes 147460
Sparse Core Ops, SparseCore 0:
  155.6 35.1 reduce-scatter.1
